TPU v7x, 32 devices: a whole 2x2x4 slice. The times are simulated.
32 devices in a mesh: dp: 8 (over z, y), tensor: 4 (over x, core).
Axes of the slice: x: 2, y: 2, z: 4, core: 2. Of those that a mesh axis runs over, the one named last changes fastest.
Arguments:
- hidden: bfloat16 [128, 4608], P('dp'), may hold values from -6 to 6
- tied_table: bfloat16 [16384, 4608], P(('dp', 'tensor')), may hold values from -0.25 to 0.25
- targets: int32 [128], P('dp'), may hold values from 0 to 16383
- loss_weight: bfloat16 [128], P('dp'), may hold values from 2 to 20
- inputs: int32 [128], P('dp'), may hold values from 0 to 16383
- embed_grad: bfloat16 [128, 4608], P('dp'), may hold values from -0.09375 to 0.09375
Outputs:
- table_grad: bfloat16 [16384, 4608], P(('dp', 'tensor'))
- hidden_grad: float32 [128, 4608], P('dp', 'tensor')
All inputs are finite; a program needn't handle non-finite values.
Results may differ from a plain program's by a relative error of at most 0.0052.
Values may be sent and summed in bfloat16 or wider, within the bound.
A program may use at most 64 MiB of HBM per device.

v0:
```python
import math
import jax
import jax.numpy as jnp
from jax import lax
from jax.sharding import PartitionSpec as P


def squashed(hidden_rows, tied_table):
    logits = lax.dot_general(
        hidden_rows, tied_table, (((1,), (1,)), ((), ())), preferred_element_type=jnp.float32
    )
    return jnp.tanh(logits / 30.0)


def per_device(hidden, tied_table, targets, loss_weight, inputs, embed_grad):
    width = hidden.shape[1]
    vocab_rows = tied_table.shape[0]
    hidden_all, grad_all, target_all, weight_all, input_all = (
        lax.all_gather(hidden, "dp", axis=0, tiled=True),
        lax.all_gather(embed_grad, "dp", axis=0, tiled=True),
        lax.all_gather(targets, "dp", axis=0, tiled=True),
        lax.all_gather(loss_weight, "dp", axis=0, tiled=True),
        lax.all_gather(inputs, "dp", axis=0, tiled=True),
    )
    offset = lax.axis_index(("dp", "tensor")) * vocab_rows
    columns = offset + jnp.arange(vocab_rows)
    squash = squashed(hidden_all, tied_table)
    expo = jnp.exp(30.0 * squash)
    total = lax.psum(jnp.sum(expo, axis=1), ("dp", "tensor"))
    hits = (target_all[:, None] == columns[None, :]).astype(jnp.float32)
    weights = weight_all.astype(jnp.float32)
    dlogit = (weights[:, None] * (expo / total[:, None] - hits) * (1.0 - squash * squash)).astype(
        jnp.bfloat16
    )
    group_rows = lax.psum_scatter(
        jnp.dot(dlogit, tied_table, preferred_element_type=jnp.float32),
        "dp",
        scatter_dimension=0,
        tiled=True,
    )
    hidden_grad = lax.psum_scatter(group_rows, "tensor", scatter_dimension=1, tiled=True)
    head_term = lax.dot_general(
        dlogit, hidden_all, (((0,), (0,)), ((), ())), preferred_element_type=jnp.float32
    )
    onehot = (input_all[None, :] == columns[:, None]).astype(jnp.bfloat16)
    embed_term = jnp.dot(onehot, grad_all, preferred_element_type=jnp.float32)
    table_grad = (head_term + math.sqrt(width) * embed_term).astype(jnp.bfloat16)
    return (table_grad, hidden_grad)


def solution(mesh):
    placed = (P("dp", None), P(("dp", "tensor"), None), P("dp"), P("dp"), P("dp"), P("dp", None))
    return jax.shard_map(
        per_device,
        mesh=mesh,
        in_specs=placed,
        out_specs=(P(("dp", "tensor"), None), P("dp", "tensor")),
        check_vma=False,
    )
```

profile of v0, /device:TPU:0, one launch (start us, length us, event | category | flops | bytes accessed | tf_op | source)
XLA Modules:
  0.0 241.8 jit_solution(12632579317556245795)
XLA Ops:
  7.2 0.0 all-gather.3.cloned.1.call-start
  7.2 0.7 all-gather.3.cloned.1.call-update
  7.9 0.0 reduce-scatter.3.cloned.1.call-start
  8.0 1.2 dynamic-slice
  9.9 0.9 dynamic-update-slice
  10.7 23.2 %all-reduce = bf16[128]{0:T(256)(128)(2,1)S(1)} all-reduce(bf16[128]{0:T(256)(128)(2,1)S(1)} %dynamic-update-slice), channel_id=1, replica_groups=mesh['dp'=8,'tensor'=4] {'dp'}, use_global_device_ids=true, to_apply=%add | all-reduce | flops 128 | bytes 512
  34.0 0.9 dynamic-update-slice.1
  34.8 0.8 dynamic-update-slice.2
  35.7 6.8 %all-reduce.3 = (s32[128]{0:T(128)S(1)}, s32[128]{0:T(128)S(1)}) all-reduce(s32[128]{0:T(128)S(1)} %dynamic-update-slice.1, s32[128]{0:T(128)S(1)} %dynamic-update-slice.2), channel_id=1, replica_groups=mesh['dp'=8,'tensor'=4] {'dp'}, use_global_device_ids=true, to_apply=%add.1 | all-reduce | flops 256 | bytes 2048
  42.5 11.3 %all-gather.3.cloned.1.call-done = bf16[128,4608]{1,0:T(8,128)(2,1)} async-done(((bf16[16,4608]{1,0:T(8,128)(2,1)}), bf16[128,4608]{1,0:T(8,128)(2,1)}) %all-gather.3.cloned.1.call-update) | async-done | bytes 1179664 | tf_op jit(solution)/shard_map/all_gather | solution.py:19
  53.8 4.4 %fusion.1 = (f32[128]{0:T(128)S(1)}, f32[128,512]{1,0:T(8,128)S(1)}) fusion(bf16[128,4608]{1,0:T(8,128)(2,1)} %all-gather.3.cloned.1.call-done, bf16[512,4608]{1,0:T(8,128)(2,1)} %param.7), kind=kOutput, calls=%fused_computation.5 | convolution fusion | flops 604176256 | bytes 6160896 | tf_op jit(solution)/shard_map/dot_general | solution.py:9
  58.3 38.7 %psum.7 = f32[128]{0:T(128)S(1)} all-reduce(f32[128]{0:T(128)S(1)} %get-tuple-element.4), channel_id=1, replica_groups=mesh['dp'=8,'tensor'=4] {'dp','tensor'}, use_global_device_ids=true, to_apply=%region_1.0 | all-reduce | flops 128 | bytes 1024 | tf_op jit(solution)/shard_map/psum | solution.py:29
  96.9 0.0 copy-start
  96.9 4.7 %fusion.5 = f32[128,4608]{1,0:T(8,128)} fusion(bf16[512,4608]{1,0:T(8,128)(2,1)} %param.7, f32[128,512]{1,0:T(8,128)S(1)} %get-tuple-element.5, s32[512]{0:T(512)S(1)} %iota_add_fusion, f32[128]{0:T(128)S(1)} %psum.7, f32[128]{0:T(128)S(1)} %convert_element_type.13, s32[128]{0:T(128)S(1)} %get-tuple-element.2), kind=kOutput, calls=%fused_computation.10 | convolution fusion | flops 604635136 | bytes 7343616 | tf_op jit(solution)/shard_map/dot_general | solution.py:36
  101.6 0.0 reduce-scatter.3.cloned.1.call-update
  101.7 0.0 all-gather.5.cloned.1.call-start
  101.7 0.7 all-gather.5.cloned.1.call-update
  102.4 0.0 reduce-scatter.5.cloned.1.call-start
  102.5 0.0 copy-done
  102.5 5.2 %fusion.6 = f32[512,4608]{1,0:T(8,128)} fusion(bf16[128,4608]{1,0:T(8,128)(2,1)S(1)} %copy-done, f32[128,512]{1,0:T(8,128)S(1)} %get-tuple-element.5, s32[512]{0:T(512)S(1)} %iota_add_fusion, f32[128]{0:T(128)S(1)} %psum.7, f32[128]{0:T(128)S(1)} %convert_element_type.13, s32[128]{0:T(128)S(1)} %get-tuple-element.2), kind=kOutput, calls=%fused_computation.11 | convolution fusion | flops 604635136 | bytes 10882560 | tf_op jit(solution)/shard_map/dot_general | solution.py:42
  107.6 63.3 %reduce-scatter.3.cloned.1.call-done = f32[16,4608]{1,0:T(8,128)} async-done(((f32[128,4608]{1,0:T(8,128)}), f32[16,4608]{1,0:T(8,128)}) %reduce-scatter.3.cloned.1.call-update) | async-done | bytes 294928 | tf_op jit(solution)/shard_map/reduce_scatter | solution.py:35
  171.0 0.0 reduce-scatter.5.cloned.1.call-update
  171.0 42.3 %all-gather.5.cloned.1.call-done = bf16[128,4608]{1,0:T(8,128)(2,1)} async-done(((bf16[16,4608]{1,0:T(8,128)(2,1)}), bf16[128,4608]{1,0:T(8,128)(2,1)}) %all-gather.5.cloned.1.call-update) | async-done | bytes 1179664 | tf_op jit(solution)/shard_map/all_gather | solution.py:20
  213.3 7.7 %add_convert_fusion = bf16[512,4608]{1,0:T(8,128)(2,1)} fusion(f32[512,4608]{1,0:T(8,128)} %fusion.6, bf16[128,4608]{1,0:T(8,128)(2,1)} %all-gather.5.cloned.1.call-done, s32[128]{0:T(128)S(1)} %get-tuple-element.3, s32[512]{0:T(512)S(1)} %iota_add_fusion), kind=kOutput, calls=%fused_computation | convolution fusion | flops 611123200 | bytes 15337984 | tf_op jit(solution)/shard_map/dot_general | solution.py:46
  220.9 14.3 %reduce-scatter.5.cloned.1.call-done = f32[16,1152]{1,0:T(8,128)} async-done(((f32[16,4608]{1,0:T(8,128)}), f32[16,1152]{1,0:T(8,128)}) %reduce-scatter.5.cloned.1.call-update) | async-done | bytes 73744 | tf_op jit(solution)/shard_map/reduce_scatter | solution.py:41
  (5 shorter events, 0.0 us)
Async XLA Ops:
  7.2 46.7 %all-gather.3.cloned.1.call-start = ((), (), s32[]{:S(2)}) async-start(), calls=%async_computation.2 | async-start | bytes 1327104 | tf_op jit(solution)/shard_map/all_gather | solution.py:19
  7.9 163.1 %reduce-scatter.3.cloned.1.call-start = ((), (), s32[]{:S(2)}) async-start(), calls=%async_computation.4 | async-start | bytes 2654208 | tf_op jit(solution)/shard_map/reduce_scatter | solution.py:35
  96.9 5.5 %copy-start = (bf16[128,4608]{1,0:T(8,128)(2,1)S(1)}, bf16[128,4608]{1,0:T(8,128)(2,1)}, u32[]{:S(2)}) copy-start(bf16[128,4608]{1,0:T(8,128)(2,1)} %all-gather.3.cloned.1.call-done) | copy-start | bytes 3538948
  101.7 111.6 %all-gather.5.cloned.1.call-start = ((), (), s32[]{:S(2)}) async-start(), calls=%async_computation.3 | async-start | bytes 1327104 | tf_op jit(solution)/shard_map/all_gather | solution.py:20
  102.4 132.9 %reduce-scatter.5.cloned.1.call-start = ((), (), s32[]{:S(2)}) async-start(), calls=%async_computation.5 | async-start | bytes 368640 | tf_op jit(solution)/shard_map/reduce_scatter | solution.py:41
Sparse Core Ops, SparseCore 0:
  10.2 43.6 all-gather.2
  101.8 69.1 reduce-scatter.2
  173.1 40.0 all-gather.4
  216.2 19.0 reduce-scatter.4
where the time goes:
time: 242 us
  waiting for transfers between devices  133 us (55%)
  blocking collectives  68.7 us (28%)
  matrix products  22 us (9%)
  between operations  14.5 us (6%)
  local copies, waits for them, and re-layouts  3.81 us (2%)
    reduce_scatter x1, waiting for transfers between devices, per_device(): lax.psum_scatter(jnp.dot(dlogit, tied_table, preferred_element_type=jnp.f...  63.3 us
    all_gather x1, waiting for transfers between devices, per_device(): lax.all_gather(embed_grad, 'dp', axis=0, tiled=True)  42.3 us
    psum x1, blocking collectives, per_device(): total = lax.psum(jnp.sum(expo, axis=1), ('dp', 'tensor'))  38.7 us
    unnamed x2, blocking collectives  30.1 us
    reduce_scatter x1, waiting for transfers between devices, per_device(): lax.psum_scatter(group_rows, 'tensor', scatter_dimension=1, tiled=True)  14.3 us
    all_gather x1, waiting for transfers between devices, per_device(): lax.all_gather(hidden, 'dp', axis=0, tiled=True)  11.3 us
    dot_general x1, matrix products, per_device(): embed_term = jnp.dot(onehot, grad_all, preferred_element_type=jnp.float32)  7.67 us
    dot_general x1, matrix products, per_device(): lax.dot_general(dlogit, hidden_all, (((0,), (0,)), ((), ())), preferred_e...  5.16 us
  transfers between devices with their start and end apart: 4, of which 4 were waited for; matrix products, arithmetic and copies ran while one was open for 7% of the time, Pallas kernels for 0%

commit v1 on v0

--- a/solution.py
+++ b/solution.py
@@ -26,7 +26,7 @@
     columns = offset + jnp.arange(vocab_rows)
     squash = squashed(hidden_all, tied_table)
     expo = jnp.exp(30.0 * squash)
-    total = lax.psum(jnp.sum(expo, axis=1), ("dp", "tensor"))
+    total = lax.psum(lax.psum(jnp.sum(expo, axis=1), "tensor"), "dp")
     hits = (target_all[:, None] == columns[None, :]).astype(jnp.float32)
     weights = weight_all.astype(jnp.float32)
     dlogit = (weights[:, None] * (expo / total[:, None] - hits) * (1.0 - squash * squash)).astype(

time: 242 us -> 226 us (0.934)
  blocking collectives: 68.7 us -> 54.9 us
  waiting for transfers between devices: 133 us -> 130 us
    psum x1 -> x2, blocking collectives: 38.7 us -> 24.8 us  [per_device(): total = lax.psum(lax.psum(jnp.sum(expo, axis=1), 'tensor'), 'dp')]
    reduce_scatter x1, waiting for transfers between devices: 63.3 us -> 60.7 us  [per_device(): lax.psum_scatter(jnp.dot(dlogit, tied_table, preferred_element_type=jnp.f...]
where the time goes in v1:
time: 226 us; the launch traced here: 225 us
  waiting for transfers between devices  130 us (58%)
  blocking collectives  54.9 us (24%)
  matrix products  22 us (10%)
  between operations  14.5 us (6%)
  local copies, waits for them, and re-layouts  3.81 us (2%)
    reduce_scatter x1, waiting for transfers between devices, per_device(): lax.psum_scatter(jnp.dot(dlogit, tied_table, preferred_element_type=jnp.f...  60.7 us
    all_gather x1, waiting for transfers between devices, per_device(): lax.all_gather(embed_grad, 'dp', axis=0, tiled=True)  42.3 us
    unnamed x2, blocking collectives  30.1 us
    psum x2, blocking collectives, per_device(): total = lax.psum(lax.psum(jnp.sum(expo, axis=1), 'tensor'), 'dp')  24.8 us
    reduce_scatter x1, waiting for transfers between devices, per_device(): lax.psum_scatter(group_rows, 'tensor', scatter_dimension=1, tiled=True)  14.3 us
    all_gather x1, waiting for transfers between devices, per_device(): lax.all_gather(hidden, 'dp', axis=0, tiled=True)  11.3 us
    dot_general x1, matrix products, per_device(): embed_term = jnp.dot(onehot, grad_all, preferred_element_type=jnp.float32)  7.67 us
    dot_general x1, matrix products, per_device(): lax.dot_general(dlogit, hidden_all, (((0,), (0,)), ((), ())), preferred_e...  5.16 us
  transfers between devices with their start and end apart: 4, of which 4 were waited for; matrix products, arithmetic and copies ran while one was open for 7% of the time, Pallas kernels for 0%

profile of v1, /device:TPU:0, one launch (start us, length us, event | category | flops | bytes accessed | tf_op | source)
XLA Modules:
  0.0 225.4 jit_solution(15398550447409349801)
XLA Ops:
  7.2 0.0 all-gather.3.cloned.1.call-start
  7.2 0.7 all-gather.3.cloned.1.call-update
  7.9 0.0 reduce-scatter.3.cloned.1.call-start
  8.0 1.2 dynamic-slice
  9.9 0.9 dynamic-update-slice
  10.7 23.2 %all-reduce = bf16[128]{0:T(256)(128)(2,1)S(1)} all-reduce(bf16[128]{0:T(256)(128)(2,1)S(1)} %dynamic-update-slice), channel_id=1, replica_groups=mesh['dp'=8,'tensor'=4] {'dp'}, use_global_device_ids=true, to_apply=%add | all-reduce | flops 128 | bytes 512
  34.0 0.9 dynamic-update-slice.1
  34.8 0.8 dynamic-update-slice.2
  35.7 6.8 %all-reduce.3 = (s32[128]{0:T(128)S(1)}, s32[128]{0:T(128)S(1)}) all-reduce(s32[128]{0:T(128)S(1)} %dynamic-update-slice.1, s32[128]{0:T(128)S(1)} %dynamic-update-slice.2), channel_id=1, replica_groups=mesh['dp'=8,'tensor'=4] {'dp'}, use_global_device_ids=true, to_apply=%add.1 | all-reduce | flops 256 | bytes 2048
  42.5 11.3 %all-gather.3.cloned.1.call-done = bf16[128,4608]{1,0:T(8,128)(2,1)} async-done(((bf16[16,4608]{1,0:T(8,128)(2,1)}), bf16[128,4608]{1,0:T(8,128)(2,1)}) %all-gather.3.cloned.1.call-update) | async-done | bytes 1179664 | tf_op jit(solution)/shard_map/all_gather | solution.py:19
  53.8 4.4 %fusion.1 = (f32[128]{0:T(128)S(1)}, f32[128,512]{1,0:T(8,128)S(1)}) fusion(bf16[128,4608]{1,0:T(8,128)(2,1)} %all-gather.3.cloned.1.call-done, bf16[512,4608]{1,0:T(8,128)(2,1)} %param.7), kind=kOutput, calls=%fused_computation.5 | convolution fusion | flops 604176256 | bytes 6160896 | tf_op jit(solution)/shard_map/dot_general | solution.py:9
  58.3 5.7 %psum.14 = f32[128]{0:T(128)S(1)} all-reduce(f32[128]{0:T(128)S(1)} %get-tuple-element.4), channel_id=1, replica_groups=mesh['dp'=8,'tensor'=4] {'tensor'}, use_global_device_ids=true, to_apply=%region_1.0 | all-reduce | flops 128 | bytes 1024 | tf_op jit(solution)/shard_map/psum | solution.py:29
  64.0 19.2 %psum.15 = f32[128]{0:T(128)S(1)} all-reduce(f32[128]{0:T(128)S(1)} %psum.14), channel_id=1, replica_groups=mesh['dp'=8,'tensor'=4] {'dp'}, use_global_device_ids=true, to_apply=%region_2.0 | all-reduce | flops 128 | bytes 1024 | tf_op jit(solution)/shard_map/psum | solution.py:29
  83.1 0.0 copy-start
  83.1 4.7 %fusion.5 = f32[128,4608]{1,0:T(8,128)} fusion(bf16[512,4608]{1,0:T(8,128)(2,1)} %param.7, f32[128,512]{1,0:T(8,128)S(1)} %get-tuple-element.5, s32[512]{0:T(512)S(1)} %iota_add_fusion, f32[128]{0:T(128)S(1)} %psum.15, f32[128]{0:T(128)S(1)} %convert_element_type.13, s32[128]{0:T(128)S(1)} %get-tuple-element.2), kind=kOutput, calls=%fused_computation.10 | convolution fusion | flops 604635136 | bytes 7343616 | tf_op jit(solution)/shard_map/dot_general | solution.py:36
  87.8 0.0 reduce-scatter.3.cloned.1.call-update
  87.9 0.0 all-gather.5.cloned.1.call-start
  87.9 0.7 all-gather.5.cloned.1.call-update
  88.6 0.0 reduce-scatter.5.cloned.1.call-start
  88.7 0.0 copy-done
  88.7 5.2 %fusion.6 = f32[512,4608]{1,0:T(8,128)} fusion(bf16[128,4608]{1,0:T(8,128)(2,1)S(1)} %copy-done, f32[128,512]{1,0:T(8,128)S(1)} %get-tuple-element.5, s32[512]{0:T(512)S(1)} %iota_add_fusion, f32[128]{0:T(128)S(1)} %psum.15, f32[128]{0:T(128)S(1)} %convert_element_type.13, s32[128]{0:T(128)S(1)} %get-tuple-element.2), kind=kOutput, calls=%fused_computation.11 | convolution fusion | flops 604635136 | bytes 10882560 | tf_op jit(solution)/shard_map/dot_general | solution.py:42
  93.8 60.7 %reduce-scatter.3.cloned.1.call-done = f32[16,4608]{1,0:T(8,128)} async-done(((f32[128,4608]{1,0:T(8,128)}), f32[16,4608]{1,0:T(8,128)}) %reduce-scatter.3.cloned.1.call-update) | async-done | bytes 294928 | tf_op jit(solution)/shard_map/reduce_scatter | solution.py:35
  154.6 0.0 reduce-scatter.5.cloned.1.call-update
  154.6 42.3 %all-gather.5.cloned.1.call-done = bf16[128,4608]{1,0:T(8,128)(2,1)} async-done(((bf16[16,4608]{1,0:T(8,128)(2,1)}), bf16[128,4608]{1,0:T(8,128)(2,1)}) %all-gather.5.cloned.1.call-update) | async-done | bytes 1179664 | tf_op jit(solution)/shard_map/all_gather | solution.py:20
  196.9 7.7 %add_convert_fusion = bf16[512,4608]{1,0:T(8,128)(2,1)} fusion(f32[512,4608]{1,0:T(8,128)} %fusion.6, bf16[128,4608]{1,0:T(8,128)(2,1)} %all-gather.5.cloned.1.call-done, s32[128]{0:T(128)S(1)} %get-tuple-element.3, s32[512]{0:T(512)S(1)} %iota_add_fusion), kind=kOutput, calls=%fused_computation | convolution fusion | flops 611123200 | bytes 15337984 | tf_op jit(solution)/shard_map/dot_general | solution.py:46
  204.6 14.3 %reduce-scatter.5.cloned.1.call-done = f32[16,1152]{1,0:T(8,128)} async-done(((f32[16,4608]{1,0:T(8,128)}), f32[16,1152]{1,0:T(8,128)}) %reduce-scatter.5.cloned.1.call-update) | async-done | bytes 73744 | tf_op jit(solution)/shard_map/reduce_scatter | solution.py:41
  (5 shorter events, 0.0 us)
Async XLA Ops:
  7.2 46.7 %all-gather.3.cloned.1.call-start = ((), (), s32[]{:S(2)}) async-start(), calls=%async_computation.2 | async-start | bytes 1327104 | tf_op jit(solution)/shard_map/all_gather | solution.py:19
  7.9 146.7 %reduce-scatter.3.cloned.1.call-start = ((), (), s32[]{:S(2)}) async-start(), calls=%async_computation.4 | async-start | bytes 2654208 | tf_op jit(solution)/shard_map/reduce_scatter | solution.py:35
  83.1 5.5 %copy-start = (bf16[128,4608]{1,0:T(8,128)(2,1)S(1)}, bf16[128,4608]{1,0:T(8,128)(2,1)}, u32[]{:S(2)}) copy-start(bf16[128,4608]{1,0:T(8,128)(2,1)} %all-gather.3.cloned.1.call-done) | copy-start | bytes 3538948
  87.9 109.0 %all-gather.5.cloned.1.call-start = ((), (), s32[]{:S(2)}) async-start(), calls=%async_computation.3 | async-start | bytes 1327104 | tf_op jit(solution)/shard_map/all_gather | solution.py:20
  88.6 130.3 %reduce-scatter.5.cloned.1.call-start = ((), (), s32[]{:S(2)}) async-start(), calls=%async_computation.5 | async-start | bytes 368640 | tf_op jit(solution)/shard_map/reduce_scatter | solution.py:41
Sparse Core Ops, SparseCore 0:
  10.2 43.6 all-gather.2
  88.0 66.5 reduce-scatter.2
  156.7 40.1 all-gather.4
  199.8 19.0 reduce-scatter.4
